TPU v7x, 256 devices: a whole 4x4x8 slice. The times are simulated.
256 devices in a mesh: lat: 32 (over z, x), lon: 2 (over core), ens: 4 (over y).
Axes of the slice: x: 4, y: 4, z: 8, core: 2. Of those that a mesh axis runs over, the one named last changes fastest.
Arguments:
- fields: bfloat16 [1024, 256, 256], P(('ens', 'lat'), 'lon'), parts along dimension 0, may hold values from -6 to 6
- lon_taps: float32 [256, 4, 9], replicated, may hold values from -2 to 2
- lat_taps: bfloat16 [256, 4, 6], P('lat'), may hold values from -2.5 to 2.5
- cycle_taps: bfloat16 [4, 8, 256], replicated, may hold values from -0.375 to 0.375
- band_start: int32 [256], P('lat'), may hold values from -4 to 254, as said below
- band_width: int32 [256], P('lat'), may hold values from 4 to 6, as said below
- mixing: bfloat16 [4, 256, 256], replicated, may hold values from -0.1875 to 0.1875
Outputs:
- layer_out: bfloat16 [1024, 256, 256], P(('ens', 'lat'), 'lon'), parts along dimension 0
There are 4 independent parts, one for each index of `ens`. A program takes and returns all parts, laid end to end along the dimension named above; an argument that names none is the same for every part. Nothing has to cross between parts.
Inputs may be any that keep to these rules, and one draw needn't show every extreme that they name: band_start[i] = i - 4 + s with s in 0 .. 3; s = 0 where i % 8 == 0 and s = 3 where i % 8 == 7. band_width[i] = 6 where i % 8 is 0 or 7.
All inputs are finite; a program needn't handle non-finite values.
Results may differ from a plain program's by a relative error of at most 0.0052.
Values may be sent and summed in bfloat16 or wider, within the bound.
A program may use at most 64 MiB of HBM per device.

v0:
```python
import jax
import jax.numpy as jnp
from jax import lax
from jax.sharding import PartitionSpec as P

HALO = 4


def extended_2(cells, sides, width, closed):
    for axis, dim in sides:
        count = lax.axis_size(axis)
        ends = count if closed else count - 1
        head = lax.slice_in_dim(cells, 0, width, axis=dim)
        tail = lax.slice_in_dim(cells, cells.shape[dim] - width, cells.shape[dim], axis=dim)
        cells = jnp.concatenate(
            [
                lax.ppermute(tail, axis, [(i, (i + 1) % count) for i in range(ends)]),
                cells,
                lax.ppermute(head, axis, [((i + 1) % count, i) for i in range(ends)]),
            ],
            axis=dim,
        )
    return cells


def toeplitz(coef, base, out_count, in_count, cycle_len):
    lead = coef.shape[:-1]
    window_len = out_count + in_count - 1
    tripled = jnp.concatenate([coef, coef, coef], axis=-1)
    begin = (base - in_count + 1) % cycle_len
    window = lax.dynamic_slice_in_dim(tripled, begin, window_len, len(lead))
    flipped = jnp.flip(window, axis=-1)
    rolled = jnp.roll(flipped, -(out_count - 1), axis=-1)
    tiled = jnp.tile(rolled, (1,) * len(lead) + (out_count,))
    cut = tiled[..., : out_count * (window_len - 1)]
    shaped = cut.reshape(lead + (out_count, window_len - 1))
    return shaped[..., :in_count]


def cycle_fold(coef, col_start, col_count, cycle_len, block_in):
    width_in = block_in.shape[1]
    circ = toeplitz(coef, col_start, col_count, width_in, cycle_len)
    return jnp.einsum("kpjm,pmc->kpjc", circ, block_in, preferred_element_type=jnp.float32)


def shards(fields, lon_taps, lat_taps, cycle_taps, band_start, band_width, mixing):
    row_count, col_count, chan_count = fields.shape
    basis_count = lon_taps.shape[1]
    reach_cells = (lon_taps.shape[2] - 1) // 2
    band_len = lat_taps.shape[2]
    polar_rows = row_count // 2
    lat_count = lax.axis_size("lat")
    lon_count = lax.axis_size("lon")
    cycle_len = lon_count * col_count
    lat_pos = lax.axis_index("lat")
    lon_pos = lax.axis_index("lon")
    ext_rows = row_count + 2 * HALO
    padded = extended_2(fields, (("lon", 1),), reach_cells, True)
    ext = extended_2(padded, (("lat", 0),), HALO, False)
    taps_padded = jnp.pad(lon_taps, ((HALO, HALO), (0, 0), (0, 0)))
    taps_here = lax.dynamic_slice_in_dim(taps_padded, lat_pos * row_count, ext_rows, 0)
    accum = jnp.zeros((basis_count, ext_rows, col_count, chan_count), jnp.float32)
    for offset in range(2 * reach_cells + 1):
        tap_now = jnp.transpose(taps_here[:, :, offset])
        accum = accum + tap_now[:, :, None, None] * ext[
            None, :, offset : offset + col_count, :
        ].astype(jnp.float32)
    filtered = accum.astype(jnp.bfloat16)
    at_top = lat_pos == 0
    at_bottom = lat_pos == lat_count - 1
    slot_start = jnp.where(at_top, 0, row_count - polar_rows).astype(jnp.int32)
    slot_rows = lax.dynamic_slice_in_dim(fields, slot_start, polar_rows, 0)
    col_start = lon_pos * col_count
    coef_start = jnp.where(at_top, 0, polar_rows).astype(jnp.int32)
    coef = lax.dynamic_slice_in_dim(cycle_taps, coef_start, polar_rows, 1)
    polar_sum = cycle_fold(
        coef, col_start, col_count, cycle_len, lax.all_gather(slot_rows, "lon", axis=1, tiled=True)
    )
    polar_z = polar_sum.astype(jnp.bfloat16)
    current = lax.dynamic_slice_in_dim(filtered, slot_start + HALO, polar_rows, 1)
    polar_here = jnp.where(at_top | at_bottom, polar_z, current)
    filtered = lax.dynamic_update_slice_in_dim(filtered, polar_here, slot_start + HALO, 1)
    base_row = lat_pos * row_count
    steps_band = jnp.arange(band_len, dtype=jnp.int32)
    target = band_start[:, None] - base_row + HALO + steps_band[None, :]
    usable = steps_band[None, :] < band_width[:, None]
    ext_ids = jnp.arange(ext_rows, dtype=jnp.int32)
    select = ((target[:, :, None] == ext_ids[None, None, :]) & usable[:, :, None]).astype(
        jnp.float32
    )
    band_matrix = jnp.einsum("lkt,lte->kle", lat_taps.astype(jnp.float32), select).astype(
        jnp.bfloat16
    )
    hidden = jnp.einsum(
        "kle,kejc->kljc", band_matrix, filtered, preferred_element_type=jnp.float32
    ).astype(jnp.bfloat16)
    mixed = jnp.einsum("kljc,kco->ljo", hidden, mixing, preferred_element_type=jnp.float32)
    return (fields.astype(jnp.float32) + mixed).astype(jnp.bfloat16)


def solution(mesh):
    in_specs = (
        P(("ens", "lat"), "lon", None),
        P(),
        P("lat", None, None),
        P(),
        P("lat"),
        P("lat"),
        P(),
    )
    out_specs = P(("ens", "lat"), "lon", None)
    return jax.shard_map(shards, mesh=mesh, in_specs=in_specs, out_specs=out_specs, check_vma=False)
```

profile of v0, /device:TPU:129, one launch (start us, length us, event | category | flops | bytes accessed | tf_op | source)
XLA Modules:
  0.0 42.9 jit_solution(14044471257622411911)
XLA Ops:
  0.0 0.0 copy-start
  0.0 0.8 %fusion.30 = (bf16[8,4,256]{2,1,0:T(4,128)(2,1)S(1)}, bf16[8,4,256]{2,1,0:T(4,128)(2,1)S(1)}) fusion(bf16[8,128,256]{2,1,0:T(8,128)(2,1)} %param.7), kind=kLoop, calls=%fused_computation.63 | loop fusion | bytes 65536 | tf_op jit(solution)/shard_map/slice | solution.py:14
  0.9 0.8 %collective-permute-start = (bf16[8,4,256]{2,1,0:T(4,128)(2,1)S(1)}, bf16[8,4,256]{2,1,0:T(4,128)(2,1)S(1)}, u32[]{:S(2)}, u32[]{:S(2)}) collective-permute-start(bf16[8,4,256]{2,1,0:T(4,128)(2,1)S(1)} %get-tuple-element.16), channel_id=1, source_target_pairs={{0,4},{4,0},{1,5},{5,1},{2,6},{6,2},{3,7},{7,3},{8,12},{12,8},{9,1... | collective-permute-start | bytes 49160 | tf_op jit(solution)/shard_map/ppermute | solution.py:17
  1.6 0.1 collective-permute-start.1
  1.7 0.7 %subtract_add_fusion = s32[8]{0:T(128)S(1)} fusion(s32[8]{0:T(128)} %param.11, s32[]{:T(128)S(6)} %mul.58), kind=kLoop, calls=%fused_computation.61 | loop fusion | flops 16 | bytes 68 | tf_op jit(solution)/shard_map/add | solution.py:85
  2.4 0.1 iota_add_fusion
  2.5 0.8 %copy.8 = bf16[8,4,6]{2,1,0:T(4,128)(2,1)S(1)} copy(bf16[8,4,6]{0,1,2:T(4,128)(2,1)} %param.9) | data formatting | bytes 768 | tf_op args[2]
  3.3 0.7 %iota_compare_fusion.1 = pred[8,6]{1,0:T(8,128)(4,1)S(1)} fusion(s32[8]{0:T(128)} %param.12), kind=kLoop, calls=%fused_computation.50 | loop fusion | flops 48 | bytes 80 | tf_op jit(solution)/shard_map/lt | solution.py:86
  4.0 0.7 %constant_dynamic-slice_fusion = bf16[4,4,256]{2,1,0:T(4,128)(2,1)S(1)} fusion(bf16[4,8,256]{2,1,0:T(8,128)(2,1)} %param.10, s32[]{:T(128)S(6)} %select_n.34), kind=kLoop, calls=%fused_computation.48 | loop fusion | bytes 16388 | tf_op jit(solution)/shard_map/dynamic_slice | solution.py:75
  4.7 0.3 fusion.9
  5.0 0.9 %fusion.20 = (f32[4,16]{1,0:T(4,128)S(1)}, f32[4,16]{1,0:T(4,128)S(1)}, f32[4,16]{1,0:T(4,128)S(1)}, f32[4,16]{1,0:T(4,128)S(1)}, f32[4,16]{1,0:T(4,128)S(1)}, /...) fusion(s32[]{:T(128)S(6)} %select_n.32, f32[256,4,9]{0,1,2:T(4,128)} %param.8, ...), kind=kLoop, calls=%fused_computation.52 | loop fusion | bytes 39204 | tf_op jit(solution)/shard_map/transpose | solution.py:64
  5.9 0.1 fusion.19
  6.0 0.2 slice.109
  6.2 0.1 slice.111
  6.3 0.0 collective-permute-done
  6.3 0.0 collective-permute-done.1
  6.4 1.2 %pad_maximum_fusion.1 = bf16[8,136,256]{2,1,0:T(8,128)(2,1)S(1)} fusion(bf16[8,4,256]{2,1,0:T(4,128)(2,1)S(1)} %collective-permute-done.1, bf16[8,128,256]{2,1,0:T(8,128)(2,1)} %param.7, bf16[8,4,256]{2,1,0:T(4,128)(2,1)S(1)} %collective-permute-done), kind=kLoop, calls=%fused_computation.25 | loop fusion | flops 1671168 | bytes 1114112 | tf_op jit(solution)/shard_map/concatenate | solution.py:15
  7.6 0.7 %fusion.29 = (bf16[4,136,256]{2,1,0:T(8,128)(2,1)}, bf16[4,136,256]{2,1,0:T(8,128)(2,1)S(1)}) fusion(bf16[8,136,256]{2,1,0:T(8,128)(2,1)S(1)} %pad_maximum_fusion.1), kind=kLoop, calls=%fused_computation.62 | loop fusion | bytes 1114112 | tf_op jit(solution)/shard_map/slice | solution.py:14
  8.3 3.1 %collective-permute-start.2 = (bf16[4,136,256]{2,1,0:T(8,128)(2,1)}, bf16[4,136,256]{2,1,0:T(8,128)(2,1)S(1)}, u32[]{:S(2)}, u32[]{:S(2)}) collective-permute-start(bf16[4,136,256]{2,1,0:T(8,128)(2,1)} %get-tuple-element.14), channel_id=1, source_target_pairs={{0,8},{8,16},{16,24},{24,32},{32,40},{40,48},{48,56},{56,64},{64,7... | collective-permute-start | bytes 835592 | tf_op jit(solution)/shard_map/ppermute | solution.py:17
  11.4 5.5 %collective-permute-start.3 = (bf16[4,136,256]{2,1,0:T(8,128)(2,1)S(1)}, bf16[4,136,256]{2,1,0:T(8,128)(2,1)S(1)}, u32[]{:S(2)}, u32[]{:S(2)}) collective-permute-start(bf16[4,136,256]{2,1,0:T(8,128)(2,1)S(1)} %get-tuple-element.15), channel_id=1, source_target_pairs={{8,0},{16,8},{24,16},{32,24},{40,32},{48,40},{56,48},{64,56},{72,6... | collective-permute-start | bytes 835592 | tf_op jit(solution)/shard_map/ppermute | solution.py:19
  16.9 0.1 tile.4
  17.1 4.0 %tile.10 = bf16[4,4,49024]{2,1,0:T(4,128)(2,1)} reshape(bf16[4,4,128,383]{3,2,1,0:T(8,128)(2,1)S(1)} %tile.4) | data formatting | bytes 3137536 | tf_op jit(solution)/shard_map/tile | solution.py:34
  21.1 0.0 slice-start
  21.1 1.4 %slice-done = bf16[4,4,48896]{2,1,0:T(4,128)(2,1)S(1)} async-done(((bf16[4,4,49024]{2,1,0:T(4,128)(2,1)}), bf16[4,4,48896]{2,1,0:T(4,128)(2,1)S(1)}, s32[]{:S(2)}) %slice-start) | async-done | bytes 1564696 | tf_op jit(solution)/shard_map/slice | solution.py:35
  22.5 0.0 copy-start.1
  22.5 4.4 %reshape.78 = bf16[4,4,128,382]{3,2,1,0:T(8,128)(2,1)} reshape(bf16[4,4,48896]{2,1,0:T(4,128)(2,1)S(1)} %slice-done) | data formatting | bytes 3129344 | tf_op jit(solution)/shard_map/reshape | solution.py:36
  26.9 0.1 copy.9
  27.0 0.0 copy-done.1
  27.1 2.8 %all_gather.3 = bf16[4,256,256]{2,1,0:T(8,128)(2,1)S(1)} all-gather(bf16[4,128,256]{2,1,0:T(8,128)(2,1)S(1)} %constant_dynamic-slice_fusion.1), channel_id=1, replica_groups=mesh['lat'=32,'lon'=2,'ens'=4] {'lon'}, dimensions={1}, use_global_device_ids=true | all-gather | bytes 786432 | tf_op jit(solution)/shard_map/all_gather | solution.py:77
  29.8 0.0 collective-permute-done.2
  29.9 0.0 collective-permute-done.3
  29.9 0.2 pad_maximum_fusion
  30.0 2.3 %slice_convert_fusion.8 = (f32[16,128,256]{2,1,0:T(8,128)S(1)}, f32[16,128,256]{2,1,0:T(8,128)S(1)}, f32[16,128,256]{2,1,0:T(8,128)S(1)}, f32[16,128,256]{2,1,0:...) fusion(bf16[16,136,256]{2,1,0:T(8,128)(2,1)S(1)} %pad_maximum_f, ...), kind=kLoop, calls=%fused_computation.24 | loop fusion | flops 4718592 | bytes 28311552 | tf_op jit(solution)/shard_map/convert_element_type | solution.py:67
  32.3 0.0 copy-start.2
  32.3 6.0 %add_convert_fusion = bf16[4,16,128,256]{3,2,1,0:T(8,128)(2,1)S(1)} fusion(f32[16,128,256]{2,1,0:T(8,128)S(1)} %get-tuple-element.6, f32[4,16]{1,0:T(4,128)S(1)} %get-tuple-element.26, f32[16,128,256]{2,1,0:T(8,128)S(1)} %get-tuple-element.7, f32[4,16]{1,0:T(4,128)S(1)} %get-tuple-element.19, f32[16,128,256]{2,1,0:T(8,128)S(1)} %get-tuple-element.8, ...), kind=kLoop, calls=%fused_computation | loop fusion | flops 37748736 | bytes 23070976 | tf_op jit(solution)/shard_map/convert_element_type | solution.py:68
  38.4 0.0 copy-done.2
  38.4 0.5 %fusion.6 = bf16[4,16,128,256]{3,2,1,0:T(8,128)(2,1)S(1)} fusion(bf16[4,16,128,256]{3,2,1,0:T(8,128)(2,1)S(1)} %add_convert_fusion, s32[]{:T(128)S(6)} %select_n.37, bf16[4,4,128,382]{3,2,1,0:T(8,128)(2,1)S(1)} %copy-done.2, pred[]{:T(512)S(6)} %or.3, bf16[4,256,256]{2,1,0:T(8,128)(2,1)S(1)} %all_gather.3), kind=kOutput, calls=%fused_computation.9 | convolution fusion | flops 269484032 | bytes 3670021 | tf_op jit(solution)/shard_map/kpjm,pmc->kpjc/dot_general | solution.py:43
  38.9 2.4 %fusion = bf16[4,8,128,256]{3,1,2,0:T(8,128)(2,1)S(1)} fusion(bf16[4,8,16,1]{2,1,3,0:T(8,128)(2,1)S(1)} %copy.9, bf16[4,16,128,256]{3,2,1,0:T(8,128)(2,1)S(1)} %fusion.6), kind=kOutput, calls=%fused_computation.2 | convolution fusion | flops 33554432 | bytes 6292480 | tf_op jit(solution)/shard_map/kle,kejc->kljc/dot_general | solution.py:94
  41.3 0.0 copy-done
  41.3 1.6 %fusion.8 = bf16[8,128,256]{2,1,0:T(8,128)(2,1)} fusion(bf16[4,8,128,256]{3,1,2,0:T(8,128)(2,1)S(1)} %fusion, bf16[8,128,256]{2,1,0:T(8,128)(2,1)S(1)} %copy-done.1, bf16[4,256,256]{2,1,0:T(8,128)(2,1)S(1)} %copy-done), kind=kOutput, calls=%fused_computation.11 | convolution fusion | flops 537657344 | bytes 3670016 | tf_op jit(solution)/shard_map/kljc,kco->ljo/dot_general | solution.py:97
  (4 shorter events, 0.0 us)
Async XLA Ops:
  0.0 41.3 %copy-start = (bf16[4,256,256]{2,1,0:T(8,128)(2,1)S(1)}, bf16[4,256,256]{2,1,0:T(8,128)(2,1)}, u32[]{:S(2)}) copy-start(bf16[4,256,256]{2,1,0:T(8,128)(2,1)} %param.13) | copy-start | bytes 1572868
  0.9 5.5 %collective-permute-start = (bf16[8,4,256]{2,1,0:T(4,128)(2,1)S(1)}, bf16[8,4,256]{2,1,0:T(4,128)(2,1)S(1)}, u32[]{:S(2)}, u32[]{:S(2)}) collective-permute-start(bf16[8,4,256]{2,1,0:T(4,128)(2,1)S(1)} %get-tuple-element.16), channel_id=1, source_target_pairs={{0,4},{4,0},{1,5},{5,1},{2,6},{6,2},{3,7},{7,3},{8,12},{12,8},{9,1... | collective-permute-start | bytes 49160 | tf_op jit(solution)/shard_map/ppermute | solution.py:17
  1.6 4.7 %collective-permute-start.1 = (bf16[8,4,256]{2,1,0:T(4,128)(2,1)S(1)}, bf16[8,4,256]{2,1,0:T(4,128)(2,1)S(1)}, u32[]{:S(2)}, u32[]{:S(2)}) collective-permute-start(bf16[8,4,256]{2,1,0:T(4,128)(2,1)S(1)} %get-tuple-element.17), channel_id=1, source_target_pairs={{4,0},{0,4},{5,1},{1,5},{6,2},{2,6},{7,3},{3,7},{12,8},{8,12},{13,... | collective-permute-start | bytes 49160 | tf_op jit(solution)/shard_map/ppermute | solution.py:19
  8.3 21.6 %collective-permute-start.2 = (bf16[4,136,256]{2,1,0:T(8,128)(2,1)}, bf16[4,136,256]{2,1,0:T(8,128)(2,1)S(1)}, u32[]{:S(2)}, u32[]{:S(2)}) collective-permute-start(bf16[4,136,256]{2,1,0:T(8,128)(2,1)} %get-tuple-element.14), channel_id=1, source_target_pairs={{0,8},{8,16},{16,24},{24,32},{32,40},{40,48},{48,56},{56,64},{64,7... | collective-permute-start | bytes 835592 | tf_op jit(solution)/shard_map/ppermute | solution.py:17
  11.4 18.4 %collective-permute-start.3 = (bf16[4,136,256]{2,1,0:T(8,128)(2,1)S(1)}, bf16[4,136,256]{2,1,0:T(8,128)(2,1)S(1)}, u32[]{:S(2)}, u32[]{:S(2)}) collective-permute-start(bf16[4,136,256]{2,1,0:T(8,128)(2,1)S(1)} %get-tuple-element.15), channel_id=1, source_target_pairs={{8,0},{16,8},{24,16},{32,24},{40,32},{48,40},{56,48},{64,56},{72,6... | collective-permute-start | bytes 835592 | tf_op jit(solution)/shard_map/ppermute | solution.py:19
  21.1 1.4 %slice-start = ((bf16[4,4,49024]{2,1,0:T(4,128)(2,1)}), bf16[4,4,48896]{2,1,0:T(4,128)(2,1)S(1)}, s32[]{:S(2)}) async-start(bf16[4,4,49024]{2,1,0:T(4,128)(2,1)} %tile.10), calls=%async_computation | async-start | bytes 3129344 | tf_op jit(solution)/shard_map/slice | solution.py:35
  22.5 4.6 %copy-start.1 = (bf16[8,128,256]{2,1,0:T(8,128)(2,1)S(1)}, bf16[8,128,256]{2,1,0:T(8,128)(2,1)}, u32[]{:S(2)}) copy-start(bf16[8,128,256]{2,1,0:T(8,128)(2,1)} %param.7) | copy-start | bytes 1572868
  32.3 6.1 %copy-start.2 = (bf16[4,4,128,382]{3,2,1,0:T(8,128)(2,1)S(1)}, bf16[4,4,128,382]{3,2,1,0:T(8,128)(2,1)}, u32[]{:S(2)}) copy-start(bf16[4,4,128,382]{3,2,1,0:T(8,128)(2,1)} %reshape.78) | copy-start | bytes 4694020
where the time goes:
time: 43.2 us; the launch traced here: 42.9 us
  local copies, waits for them, and re-layouts  14.5 us (34%)
  other arithmetic  11.3 us (26%)
  starting transfers between devices  9.45 us (22%)
  matrix products  4.73 us (11%)
  blocking collectives  2.78 us (6%)
    convert_element_type x1, other arithmetic, shards(): filtered = accum.astype(jnp.bfloat16)  6.03 us
    ppermute x2, starting transfers between devices, extended_2(): lax.ppermute(head, axis, [((i + 1) % count, i) for i in range(ends)])  5.59 us
    reshape x1, local copies, waits for them, and re-layouts, toeplitz(): shaped = cut.reshape(lead + (out_count, window_len - 1))  4.44 us
    another operation x2, local copies, waits for them, and re-layouts, toeplitz(): tiled = jnp.tile(rolled, (1,) * len(lead) + (out_count,))  4.13 us
    ppermute x2, starting transfers between devices, extended_2(): lax.ppermute(tail, axis, [(i, (i + 1) % count) for i in range(ends)])  3.86 us
    all_gather x1, blocking collectives, shards(): lax.all_gather(slot_rows, 'lon', axis=1, tiled=True)  2.78 us
    dot_general x1, matrix products, shards(): jnp.einsum('kle,kejc->kljc', band_matrix, filtered, preferred_element_typ...  2.38 us
    convert_element_type x1, other arithmetic, shards(): accum = accum + tap_now[:, :, None, None] * ext[None, :, offset:offset +...  2.3 us
  transfers between devices with their start and end apart: 4, of which 0 were waited for; matrix products, arithmetic and copies ran while one was open for 31% of the time, Pallas kernels for 0%

commit v1 on v0

--- a/solution.py
+++ b/solution.py
@@ -2,6 +2,7 @@
 import jax.numpy as jnp
 from jax import lax
 from jax.sharding import PartitionSpec as P
+from jax.lax import all_to_all, axis_size
 
 HALO = 4
 
@@ -74,7 +75,13 @@
     coef_start = jnp.where(at_top, 0, polar_rows).astype(jnp.int32)
     coef = lax.dynamic_slice_in_dim(cycle_taps, coef_start, polar_rows, 1)
     polar_sum = cycle_fold(
-        coef, col_start, col_count, cycle_len, lax.all_gather(slot_rows, "lon", axis=1, tiled=True)
+        coef,
+        col_start,
+        col_count,
+        cycle_len,
+        jnp.concatenate(
+            all_to_all(jnp.stack([slot_rows for _ in range(axis_size("lon"))], 0), "lon", 0, 0), 1
+        ),
     )
     polar_z = polar_sum.astype(jnp.bfloat16)
     current = lax.dynamic_slice_in_dim(filtered, slot_start + HALO, polar_rows, 1)

time: 43.2 us -> 88.2 us (2.04)
  local copies, waits for them, and re-layouts: 14.5 us -> 47.1 us
  other arithmetic: 11.3 us -> 19.4 us
  starting transfers between devices: 9.45 us -> 13.3 us
  blocking collectives: 2.78 us -> 0 us
  matrix products: 4.73 us -> 7.42 us
    convert_element_type x1 -> x9, local copies, waits for them, and re-layouts: 0.12 us -> 25.1 us  [shards(): accum = accum + tap_now[:, :, None, None] * ext[None, :, offset:offset +...]
    dynamic_update_slice x0 -> x1, local copies, waits for them, and re-layouts: none -> 7.91 us  [shards(): lax.dynamic_update_slice_in_dim(filtered, polar_here, slot_start + HALO, 1)]
    convert_element_type x1, other arithmetic: 6.03 us -> 11.1 us  [shards(): filtered = accum.astype(jnp.bfloat16)]
    all_to_all x0 -> x1, starting transfers between devices: none -> 3.89 us  [shards(): all_to_all(jnp.stack([slot_rows for _ in range(axis_size('lon'))], 0), 'l...]
    convert_element_type x1, other arithmetic: 2.3 us -> 5.92 us  [shards(): accum = accum + tap_now[:, :, None, None] * ext[None, :, offset:offset +...]
    all_gather x1 -> x0, blocking collectives: 2.78 us -> none  [shards(): lax.all_gather(slot_rows, 'lon', axis=1, tiled=True)]
    dot_general x1, matrix products: 0.5 us -> 2.79 us  [cycle_fold(): jnp.einsum('kpjm,pmc->kpjc', circ, block_in, preferred_element_type=jnp.f...]
    another operation x0 -> x1, local copies, waits for them, and re-layouts: none -> 0.97 us  [shards(): jnp.stack([slot_rows for _ in range(axis_size('lon'))], 0)]
  transfers between devices with their start and end apart: 4 -> 5, of which waited for: 0 -> 0; matrix products, arithmetic and copies ran while one was open for 31% -> 15% of each run, Pallas kernels for 0% -> 0%
where the time goes in v1:
time: 88.2 us; the launch traced here: 87.5 us
  local copies, waits for them, and re-layouts  47.1 us (53%)
  other arithmetic  19.4 us (22%)
  starting transfers between devices  13.3 us (15%)
  matrix products  7.42 us (8%)
    convert_element_type x9, local copies, waits for them, and re-layouts, shards(): accum = accum + tap_now[:, :, None, None] * ext[None, :, offset:offset +...  25.1 us
    convert_element_type x1, other arithmetic, shards(): filtered = accum.astype(jnp.bfloat16)  11.1 us
    dynamic_update_slice x1, local copies, waits for them, and re-layouts, shards(): lax.dynamic_update_slice_in_dim(filtered, polar_here, slot_start + HALO, 1)  7.91 us
    convert_element_type x1, other arithmetic, shards(): accum = accum + tap_now[:, :, None, None] * ext[None, :, offset:offset +...  5.92 us
    ppermute x2, starting transfers between devices, extended_2(): lax.ppermute(head, axis, [((i + 1) % count, i) for i in range(ends)])  5.58 us
    reshape x1, local copies, waits for them, and re-layouts, toeplitz(): shaped = cut.reshape(lead + (out_count, window_len - 1))  4.43 us
    another operation x2, local copies, waits for them, and re-layouts, toeplitz(): tiled = jnp.tile(rolled, (1,) * len(lead) + (out_count,))  4.1 us
    all_to_all x1, starting transfers between devices, shards(): all_to_all(jnp.stack([slot_rows for _ in range(axis_size('lon'))], 0), 'l...  3.89 us
  transfers between devices with their start and end apart: 5, of which 0 were waited for; matrix products, arithmetic and copies ran while one was open for 15% of the time, Pallas kernels for 0%

profile of v1, /device:TPU:129, one launch (start us, length us, event | category | flops | bytes accessed | tf_op | source)
XLA Modules:
  0.0 87.5 jit_solution(10823349165216634524)
XLA Ops:
  0.0 0.0 copy-start
  0.0 0.0 copy-start.7
  0.0 0.0 copy-start.8
  0.0 0.9 %fusion.34 = (bf16[8,4,256]{2,1,0:T(4,128)(2,1)S(1)}, bf16[8,4,256]{2,1,0:T(4,128)(2,1)S(1)}) fusion(bf16[8,128,256]{2,1,0:T(8,128)(2,1)} %param.7), kind=kLoop, calls=%fused_computation.62 | loop fusion | bytes 65536 | tf_op jit(solution)/shard_map/slice | solution.py:15
  0.9 0.8 collective-permute-start
  1.7 0.1 collective-permute-start.1
  1.8 1.0 %dynamic-slice_bitcast_fusion = bf16[1,4,128,256]{3,2,1,0:T(8,128)(2,1)S(1)} fusion(bf16[8,128,256]{2,1,0:T(8,128)(2,1)} %param.7, s32[]{:T(128)S(6)} %select_n.34), kind=kLoop, calls=%fused_computation.27 | loop fusion | bytes 524292 | tf_op jit(solution)/shard_map/stack | solution.py:83
  2.7 0.8 pad_maximum_fusion.2
  3.6 3.9 %all-to-all-start = ((bf16[2,4,128,256]{3,2,1,0:T(8,128)(2,1)}), bf16[2,4,128,256]{3,2,1,0:T(8,128)(2,1)S(1)}, u32[]{:S(2)}, u32[]{:S(2)}) async-start(bf16[2,4,128,256]{3,2,1,0:T(8,128)(2,1)} %pad_maximum_fusion.2), calls=%async_computation | async-start | bytes 1048576 | tf_op jit(solution)/shard_map/all_to_all | solution.py:83
  7.5 0.0 copy-done.7
  7.5 0.1 iota_add_fusion
  7.6 0.1 iota_compare_fusion.1
  7.6 0.1 fusion.22
  7.8 0.2 slice.109
  8.0 0.1 slice.111
  8.1 0.0 collective-permute-done
  8.1 0.0 collective-permute-done.1
  8.1 0.1 pad_maximum_fusion.1
  8.3 0.9 fusion.33
  9.1 3.1 %collective-permute-start.2 = (bf16[4,136,256]{2,1,0:T(8,128)(2,1)}, bf16[4,136,256]{2,1,0:T(8,128)(2,1)S(1)}, u32[]{:S(2)}, u32[]{:S(2)}) collective-permute-start(bf16[4,136,256]{2,1,0:T(8,128)(2,1)} %get-tuple-element.14), channel_id=1, source_target_pairs={{0,8},{8,16},{16,24},{24,32},{32,40},{40,48},{48,56},{56,64},{64,7... | collective-permute-start | bytes 835592 | tf_op jit(solution)/shard_map/ppermute | solution.py:18
  12.3 5.5 %collective-permute-start.3 = (bf16[4,136,256]{2,1,0:T(8,128)(2,1)}, bf16[4,136,256]{2,1,0:T(8,128)(2,1)}, u32[]{:S(2)}, u32[]{:S(2)}) collective-permute-start(bf16[4,136,256]{2,1,0:T(8,128)(2,1)} %get-tuple-element.15), channel_id=1, source_target_pairs={{8,0},{16,8},{24,16},{32,24},{40,32},{48,40},{56,48},{64,56},{72,6... | collective-permute-start | bytes 835592 | tf_op jit(solution)/shard_map/ppermute | solution.py:20
  17.8 0.1 tile.4
  17.9 4.0 %tile.10 = bf16[4,4,49024]{2,1,0:T(4,128)(2,1)} reshape(bf16[4,4,128,383]{3,2,1,0:T(8,128)(2,1)S(1)} %tile.4) | data formatting | bytes 3137536 | tf_op jit(solution)/shard_map/tile | solution.py:35
  21.9 1.4 %slice-done = bf16[4,4,48896]{2,1,0:T(4,128)(2,1)S(1)} async-done(((bf16[4,4,49024]{2,1,0:T(4,128)(2,1)}), bf16[4,4,48896]{2,1,0:T(4,128)(2,1)S(1)}, s32[]{:S(2)}) %slice-start) | async-done | bytes 1564696 | tf_op jit(solution)/shard_map/slice | solution.py:36
  23.3 4.4 %reshape.86 = bf16[4,4,128,382]{3,2,1,0:T(8,128)(2,1)} reshape(bf16[4,4,48896]{2,1,0:T(4,128)(2,1)S(1)} %slice-done) | data formatting | bytes 3129344 | tf_op jit(solution)/shard_map/reshape | solution.py:37
  27.7 0.1 copy.8
  27.8 0.0 all-to-all-done
  27.8 0.8 copy.18
  28.7 0.1 fusion.24
  28.8 0.2 fusion.14
  29.0 0.0 collective-permute-done.2
  29.0 0.0 collective-permute-done.3
  29.0 1.1 %pad_maximum_fusion = bf16[16,136,256]{2,1,0:T(8,128)(2,1)S(1)} fusion(bf16[4,136,256]{2,1,0:T(8,128)(2,1)} %collective-permute-done.3, bf16[8,4,256]{2,1,0:T(4,128)(2,1)S(1)} %collective-permute-done.1, bf16[8,128,256]{2,1,0:T(8,128)(2,1)S(1)} %copy-done.1, bf16[8,4,256]{2,1,0:T(4,128)(2,1)S(1)} %collective-permute-done, ...), kind=kLoop, calls=%fused_computation.11 | loop fusion | flops 5570560 | bytes 2228224 | tf_op jit(solution)/shard_map/concatenate | solution.py:16
  30.1 5.9 %slice_convert_fusion.8 = (f32[16,128,256]{2,1,0:T(8,128)S(1)}, f32[16,128,256]{2,1,0:T(8,128)}, f32[16,128,256]{2,1,0:T(8,128)}, f32[16,128,256]{2,1,0:T(8,128)...) fusion(bf16[16,136,256]{2,1,0:T(8,128)(2,1)S(1)} %pad_maximum_f, ...), kind=kLoop, calls=%fused_computation.23 | loop fusion | flops 4718592 | bytes 28311552 | tf_op jit(solution)/shard_map/convert_element_type | solution.py:68
  36.0 2.9 %copy.10 = f32[16,128,256]{1,2,0:T(8,128)} copy(f32[16,128,256]{2,1,0:T(8,128)} %get-tuple-element.13) | data formatting | bytes 4194304 | tf_op jit(solution)/shard_map/convert_element_type | solution.py:68
  38.9 2.9 %copy.11 = f32[16,128,256]{1,2,0:T(8,128)} copy(f32[16,128,256]{2,1,0:T(8,128)} %get-tuple-element.12) | data formatting | bytes 4194304 | tf_op jit(solution)/shard_map/convert_element_type | solution.py:68
  41.9 2.9 %copy.12 = f32[16,128,256]{1,2,0:T(8,128)} copy(f32[16,128,256]{2,1,0:T(8,128)} %get-tuple-element.11) | data formatting | bytes 4194304 | tf_op jit(solution)/shard_map/convert_element_type | solution.py:68
  44.8 2.9 %copy.13 = f32[16,128,256]{1,2,0:T(8,128)} copy(f32[16,128,256]{2,1,0:T(8,128)} %get-tuple-element.10) | data formatting | bytes 4194304 | tf_op jit(solution)/shard_map/convert_element_type | solution.py:68
  47.7 2.9 %copy.14 = f32[16,128,256]{1,2,0:T(8,128)} copy(f32[16,128,256]{2,1,0:T(8,128)} %get-tuple-element.9) | data formatting | bytes 4194304 | tf_op jit(solution)/shard_map/convert_element_type | solution.py:68
  50.6 2.9 %copy.15 = f32[16,128,256]{1,2,0:T(8,128)} copy(f32[16,128,256]{2,1,0:T(8,128)} %get-tuple-element.8) | data formatting | bytes 4194304 | tf_op jit(solution)/shard_map/convert_element_type | solution.py:68
  53.5 2.9 %copy.16 = f32[16,128,256]{1,2,0:T(8,128)} copy(f32[16,128,256]{2,1,0:T(8,128)} %get-tuple-element.7) | data formatting | bytes 4194304 | tf_op jit(solution)/shard_map/convert_element_type | solution.py:68
  56.4 2.9 %copy.17 = f32[16,128,256]{1,2,0:T(8,128)} copy(f32[16,128,256]{2,1,0:T(8,128)} %get-tuple-element.6) | data formatting | bytes 4194304 | tf_op jit(solution)/shard_map/convert_element_type | solution.py:68
  59.3 1.8 %copy.9 = f32[16,128,256]{1,2,0:T(8,128)} copy(f32[16,128,256]{2,1,0:T(8,128)S(1)} %get-tuple-element.5) | data formatting | bytes 4194304 | tf_op jit(solution)/shard_map/convert_element_type | solution.py:68
  61.2 11.1 %add_convert_fusion = bf16[4,16,128,256]{2,3,1,0:T(8,128)(2,1)} fusion(f32[16,128,256]{1,2,0:T(8,128)} %copy.17, f32[4,16]{1,0:T(4,128)S(1)} %get-tuple-element.26, f32[16,128,256]{1,2,0:T(8,128)} %copy.16, f32[4,16]{1,0:T(4,128)S(1)} %get-tuple-element.19, f32[16,128,256]{1,2,0:T(8,128)} %copy.15, f32[4,16]{1,0:T(4,128)S(1)} %get-tuple-element.20, ...), kind=kLoop, calls=%fused_computation | loop fusion | flops 37748736 | bytes 23070976 | tf_op jit(solution)/shard_map/convert_element_type | solution.py:69
  72.3 2.8 %fusion.7 = bf16[4,16,128,256]{2,3,1,0:T(8,128)(2,1)} fusion(bf16[4,16,128,256]{2,3,1,0:T(8,128)(2,1)} %add_convert_fusion, s32[]{:T(128)S(6)} %select_n.37, bf16[4,256,256,1]{2,1,0,3:T(8,128)(2,1)S(1)} %bitcast.68, bf16[4,4,128,382]{3,2,1,0:T(8,128)(2,1)S(1)} %copy-done.2, pred[]{:T(512)S(6)} %or.3), kind=kOutput, calls=%fused_computation.8 | convolution fusion | flops 269484032 | bytes 3670021 | tf_op jit(solution)/shard_map/kpjm,pmc->kpjc/dot_general | solution.py:44
  75.1 7.9 %copy.21 = bf16[4,16,128,256]{3,1,2,0:T(8,128)(2,1)} copy(bf16[4,16,128,256]{2,3,1,0:T(8,128)(2,1)} %fusion.7) | data formatting | bytes 8388608 | tf_op jit(solution)/shard_map/dynamic_update_slice | solution.py:89
  83.0 2.9 %convolution_convert_fusion = bf16[4,8,128,256]{3,1,2,0:T(8,128)(2,1)S(1)} fusion(bf16[4,16,128,256]{3,1,2,0:T(8,128)(2,1)} %copy.21, bf16[4,8,16,1]{2,0,1,3:T(4,128)(2,1)S(1)} %fusion.14), kind=kOutput, calls=%fused_computation.3 | convolution fusion | flops 34603008 | bytes 6292480 | tf_op jit(solution)/shard_map/kle,kejc->kljc/dot_general | solution.py:101
  85.9 1.6 %fusion.11 = bf16[8,128,256]{2,1,0:T(8,128)(2,1)} fusion(bf16[4,8,128,256]{3,1,2,0:T(8,128)(2,1)S(1)} %convolution_convert_fusion, bf16[8,128,256]{2,1,0:T(8,128)(2,1)S(1)} %copy-done.1, bf16[4,256,256]{2,1,0:T(8,128)(2,1)S(1)} %copy-done), kind=kOutput, calls=%fused_computation.10 | convolution fusion | flops 537657344 | bytes 3670016 | tf_op jit(solution)/shard_map/kljc,kco->ljo/dot_general | solution.py:104
  (20 shorter events, 0.1 us)
Async XLA Ops:
  0.0 85.9 %copy-start = (bf16[4,256,256]{2,1,0:T(8,128)(2,1)S(1)}, bf16[4,256,256]{2,1,0:T(8,128)(2,1)}, u32[]{:S(2)}) copy-start(bf16[4,256,256]{2,1,0:T(8,128)(2,1)} %param.13) | copy-start | bytes 1572868
  0.0 8.1 %copy-start.1 = (bf16[8,128,256]{2,1,0:T(8,128)(2,1)S(1)}, bf16[8,128,256]{2,1,0:T(8,128)(2,1)}, u32[]{:S(2)}) copy-start(bf16[8,128,256]{2,1,0:T(8,128)(2,1)} %param.7) | copy-start | bytes 1572868
  0.0 7.5 %copy-start.6 = (bf16[4,8,256]{2,1,0:T(8,128)(2,1)S(1)}, bf16[4,8,256]{2,1,0:T(8,128)(2,1)}, u32[]{:S(2)}) copy-start(bf16[4,8,256]{2,1,0:T(8,128)(2,1)} %param.10) | copy-start | bytes 49156
  0.0 7.5 %copy-start.7 = (s32[8]{0:T(128)S(1)}, s32[8]{0:T(128)}, u32[]{:S(2)}) copy-start(s32[8]{0:T(128)} %param.11) | copy-start | bytes 100
  0.0 7.6 %copy-start.8 = (s32[8]{0:T(128)S(1)}, s32[8]{0:T(128)}, u32[]{:S(2)}) copy-start(s32[8]{0:T(128)} %param.12) | copy-start | bytes 100
  0.9 7.2 %collective-permute-start = (bf16[8,4,256]{2,1,0:T(4,128)(2,1)S(1)}, bf16[8,4,256]{2,1,0:T(4,128)(2,1)S(1)}, u32[]{:S(2)}, u32[]{:S(2)}) collective-permute-start(bf16[8,4,256]{2,1,0:T(4,128)(2,1)S(1)} %get-tuple-element.16), channel_id=1, source_target_pairs={{0,4},{4,0},{1,5},{5,1},{2,6},{6,2},{3,7},{7,3},{8,12},{12,8},{9,1... | collective-permute-start | bytes 49160 | tf_op jit(solution)/shard_map/ppermute | solution.py:18
  1.7 6.4 %collective-permute-start.1 = (bf16[8,4,256]{2,1,0:T(4,128)(2,1)S(1)}, bf16[8,4,256]{2,1,0:T(4,128)(2,1)S(1)}, u32[]{:S(2)}, u32[]{:S(2)}) collective-permute-start(bf16[8,4,256]{2,1,0:T(4,128)(2,1)S(1)} %get-tuple-element.17), channel_id=1, source_target_pairs={{4,0},{0,4},{5,1},{1,5},{6,2},{2,6},{7,3},{3,7},{12,8},{8,12},{13,... | collective-permute-start | bytes 49160 | tf_op jit(solution)/shard_map/ppermute | solution.py:20
  3.6 24.3 %all-to-all-start = ((bf16[2,4,128,256]{3,2,1,0:T(8,128)(2,1)}), bf16[2,4,128,256]{3,2,1,0:T(8,128)(2,1)S(1)}, u32[]{:S(2)}, u32[]{:S(2)}) async-start(bf16[2,4,128,256]{3,2,1,0:T(8,128)(2,1)} %pad_maximum_fusion.2), calls=%async_computation | async-start | bytes 1048576 | tf_op jit(solution)/shard_map/all_to_all | solution.py:83
  9.1 19.8 %collective-permute-start.2 = (bf16[4,136,256]{2,1,0:T(8,128)(2,1)}, bf16[4,136,256]{2,1,0:T(8,128)(2,1)S(1)}, u32[]{:S(2)}, u32[]{:S(2)}) collective-permute-start(bf16[4,136,256]{2,1,0:T(8,128)(2,1)} %get-tuple-element.14), channel_id=1, source_target_pairs={{0,8},{8,16},{16,24},{24,32},{32,40},{40,48},{48,56},{56,64},{64,7... | collective-permute-start | bytes 835592 | tf_op jit(solution)/shard_map/ppermute | solution.py:18
  12.3 16.7 %collective-permute-start.3 = (bf16[4,136,256]{2,1,0:T(8,128)(2,1)}, bf16[4,136,256]{2,1,0:T(8,128)(2,1)}, u32[]{:S(2)}, u32[]{:S(2)}) collective-permute-start(bf16[4,136,256]{2,1,0:T(8,128)(2,1)} %get-tuple-element.15), channel_id=1, source_target_pairs={{8,0},{16,8},{24,16},{32,24},{40,32},{48,40},{56,48},{64,56},{72,6... | collective-permute-start | bytes 835592 | tf_op jit(solution)/shard_map/ppermute | solution.py:20
  21.9 1.4 %slice-start = ((bf16[4,4,49024]{2,1,0:T(4,128)(2,1)}), bf16[4,4,48896]{2,1,0:T(4,128)(2,1)S(1)}, s32[]{:S(2)}) async-start(bf16[4,4,49024]{2,1,0:T(4,128)(2,1)} %tile.10), calls=%async_computation.1 | async-start | bytes 3129344 | tf_op jit(solution)/shard_map/slice | solution.py:36
  23.3 4.4 %copy-start.5 = (bf16[8,4,6]{0,1,2:T(4,128)(2,1)S(1)}, bf16[8,4,6]{0,1,2:T(4,128)(2,1)}, u32[]{:S(2)}) copy-start(bf16[8,4,6]{0,1,2:T(4,128)(2,1)} %param.9) | copy-start | bytes 1156
  23.3 5.4 %copy-start.4 = (f32[256,4,9]{0,1,2:T(4,128)S(1)}, f32[256,4,9]{0,1,2:T(4,128)}, u32[]{:S(2)}) copy-start(f32[256,4,9]{0,1,2:T(4,128)} %param.8) | copy-start | bytes 110596
  61.2 11.2 %copy-start.2 = (bf16[4,4,128,382]{3,2,1,0:T(8,128)(2,1)S(1)}, bf16[4,4,128,382]{3,2,1,0:T(8,128)(2,1)}, u32[]{:S(2)}) copy-start(bf16[4,4,128,382]{3,2,1,0:T(8,128)(2,1)} %reshape.86) | copy-start | bytes 4694020
  61.2 11.2 %copy-start.3 = (bf16[2,4,128,256]{3,2,0,1:T(8,128)(2,1)S(1)}, bf16[2,4,128,256]{3,2,0,1:T(8,128)(2,1)}, u32[]{:S(2)}) copy-start(bf16[2,4,128,256]{3,2,0,1:T(8,128)(2,1)} %copy.18) | copy-start | bytes 1572868
